TPU v7x, 128 devices: a whole 4x4x4 slice. The times are simulated.
128 devices in a mesh: store: 8 (over z, core), mp: 16 (over y, x).
Axes of the slice: x: 4, y: 4, z: 4, core: 2. Of those that a mesh axis runs over, the one named last changes fastest.
Arguments:
- tokens: bfloat16 [2048, 6144], P('store', 'mp'), may hold values from -6 to 6
- gain: float32 [6144], replicated, may hold values from 0.1 to 1.9
- base_projection_weight: bfloat16 [6144, 6144], P(None, 'mp'), may hold values from -0.078125 to 0.078125
- adapter_down_weight: bfloat16 [64, 64, 6144], P('store', None, 'mp'), may hold values from -0.078125 to 0.078125
- adapter_up_weight: bfloat16 [64, 64, 6144], P('store', None, 'mp'), may hold values from -0.75 to 0.75
- plan: int32 [8, 4], replicated, may hold values from 0 to 63, as said below
- target: int32 [2048, 1], P('store'), may hold values from 0 to 7; in each aligned block of 256 rows (0 to 255, 256 to 511, ...) at most 64 rows name the same one
- slot: int32 [2048], P('store'), may hold values from 0 to 11
Outputs:
- hidden_out: bfloat16 [2048, 6144], P('store', 'mp')
Inputs may be any that keep to these rules, and one draw needn't show every extreme that they name: plan[g, r] is an adapter owned by a store group other than g; adapter a is owned by group a // 8. `target`: among the 256 rows of one store group at most 64 name the same group, a bound that some block reaches.
All inputs are finite; a program needn't handle non-finite values.
Results may differ from a plain program's by a relative error of at most 0.0063.
Values may be sent and summed in bfloat16 or wider, within the bound.
A program may use at most 64 MiB of HBM per device.

v0:
```python
import jax
import jax.numpy as jnp
from jax import lax
from jax.sharding import PartitionSpec as P

STEPS = 4
CAP = 64
adapter_scale = 0.5


def local(
    tokens, gain, base_projection_weight, adapter_down_weight, adapter_up_weight, plan, target, slot
):
    store_count = lax.axis_size("store")
    group = lax.axis_index("store")
    owned_adapters = adapter_down_weight.shape[0]
    rank_position = adapter_down_weight.shape[1]
    width_portion = adapter_down_weight.shape[2]
    replica_count = plan.shape[1]
    n_slots = owned_adapters + replica_count
    flattened_down = adapter_down_weight.reshape(owned_adapters, rank_position * width_portion)
    flattened_up = adapter_up_weight.reshape(owned_adapters, rank_position * width_portion)
    own_plan = lax.dynamic_slice_in_dim(plan, group, 1, 0)[0]
    pieces = (
        lax.all_gather(flattened_down, "store", axis=0, tiled=True),
        lax.all_gather(flattened_up, "store", axis=0, tiled=True),
    )
    count = pieces[0].shape[0]
    select = (own_plan[:, None] == jnp.arange(count, dtype=jnp.int32)[None, :]).astype(jnp.bfloat16)
    replica_down_factor = jnp.dot(select, pieces[0], preferred_element_type=jnp.float32)
    replica_up_factor = jnp.dot(select, pieces[1], preferred_element_type=jnp.float32)
    host_down = jnp.concatenate(
        [
            adapter_down_weight,
            replica_down_factor.astype(jnp.bfloat16).reshape(
                replica_count, rank_position, width_portion
            ),
        ],
        0,
    )
    host_down = host_down.reshape(n_slots * rank_position, width_portion)
    host_up = jnp.concatenate(
        [
            adapter_up_weight,
            replica_up_factor.astype(jnp.bfloat16).reshape(
                replica_count, rank_position, width_portion
            ),
        ],
        0,
    )
    host_up = host_up.reshape(n_slots * rank_position, width_portion)
    target_group = target[:, 0]
    member = (target_group[:, None] == jnp.arange(store_count, dtype=jnp.int32)[None, :]).astype(
        jnp.int32
    )
    earlier = jnp.cumsum(member, axis=0) - member
    bucket_place = jnp.sum(earlier * member, axis=1)
    row_index = target_group * CAP + bucket_place
    slot_buffer = (
        jnp.full((store_count * CAP,), -1, jnp.int32)
        .at[row_index]
        .set(slot)
        .reshape(store_count, CAP)
    )
    state = tokens
    column_start = lax.axis_index("mp") * width_portion
    for step in range(STEPS):
        whole = lax.all_gather(state, "mp", axis=1, tiled=True)
        values = whole.astype(jnp.float32)
        mean_sq = jnp.mean(values * values, axis=1, keepdims=True)
        normed = (values * lax.rsqrt(mean_sq + 1e-05) * gain[None, :]).astype(jnp.bfloat16)
        mine = lax.dynamic_slice_in_dim(normed, column_start, width_portion, 1)
        row_buffer = (
            jnp.zeros((store_count * CAP, width_portion), jnp.bfloat16).at[row_index].set(mine)
        )
        row_buffer = row_buffer.reshape(store_count, CAP, width_portion)
        rows = lax.all_to_all(row_buffer, "store", split_axis=0, concat_axis=0, tiled=True)
        slots_in = lax.all_to_all(slot_buffer, "store", split_axis=0, concat_axis=0, tiled=True)
        senders, adapter_count = slots_in.shape
        total_rows = senders * adapter_count
        flat_rows = rows.reshape(total_rows, width_portion)
        partial_value = lax.dot_general(
            flat_rows, host_down, (((1,), (1,)), ((), ())), preferred_element_type=jnp.float32
        )
        selected_adapter = (
            slots_in.reshape(total_rows)[:, None] == jnp.arange(n_slots, dtype=jnp.int32)[None, :]
        )
        partial_value = jnp.sum(
            partial_value.reshape(total_rows, n_slots, rank_position)
            * selected_adapter[:, :, None].astype(jnp.float32),
            axis=1,
        )
        summed_share = lax.psum_scatter(
            partial_value, "mp", scatter_dimension=0, tiled=True
        ).astype(jnp.bfloat16)
        inner = lax.all_gather(summed_share, "mp", axis=0, tiled=True)
        spread_rows = (
            selected_adapter[:, :, None].astype(jnp.bfloat16) * inner[:, None, :]
        ).reshape(total_rows, n_slots * rank_position)
        outer = jnp.dot(spread_rows, host_up, preferred_element_type=jnp.float32)
        outer = (
            (adapter_scale * outer)
            .astype(jnp.bfloat16)
            .reshape(senders, adapter_count, width_portion)
        )
        returned = lax.all_to_all(outer, "store", split_axis=0, concat_axis=0, tiled=True)
        delta = returned.reshape(store_count * CAP, width_portion)[row_index]
        base = jnp.dot(normed, base_projection_weight, preferred_element_type=jnp.float32)
        state = (state.astype(jnp.float32) + base + delta.astype(jnp.float32)).astype(jnp.bfloat16)
    return state


def solution(mesh):
    return jax.shard_map(
        local,
        mesh=mesh,
        in_specs=(
            P("store", "mp"),
            P(),
            P(None, "mp"),
            P("store", None, "mp"),
            P("store", None, "mp"),
            P(),
            P("store", None),
            P("store"),
        ),
        out_specs=P("store", "mp"),
        check_vma=False,
    )
```

profile of v0, /device:TPU:1, one launch (start us, length us, event | category | flops | bytes accessed | tf_op | source)
XLA Modules:
  0.0 813.4 jit_solution(17470650637500841050)
XLA Ops:
  16.6 6.8 all-to-all-start
  29.9 33.1 %all-gather.7.cloned.1.call-done = bf16[256,6144]{1,0:T(8,128)(2,1)} async-done(((bf16[256,384]{1,0:T(8,128)(2,1)}), bf16[256,6144]{1,0:T(8,128)(2,1)}) %all-gather.7.cloned.1.call-update) | async-done | bytes 3145744 | tf_op jit(solution)/shard_map/all_gather | solution.py:68
  63.0 2.7 fusion
  69.9 6.5 all-to-all-start.1
  76.4 21.6 %all-gather.9.cloned.1.call-done = bf16[64,24576]{1,0:T(8,128)(2,1)} async-done(((bf16[8,24576]{1,0:T(8,128)(2,1)}), bf16[64,24576]{1,0:T(8,128)(2,1)}) %all-gather.9.cloned.1.call-update) | async-done | bytes 3145744 | tf_op jit(solution)/shard_map/all_gather | solution.py:25
  105.3 20.9 %all-gather.11.cloned.1.call-done = bf16[64,24576]{1,0:T(8,128)(2,1)} async-done(((bf16[8,24576]{1,0:T(8,128)(2,1)}), bf16[64,24576]{1,0:T(8,128)(2,1)}) %all-gather.11.cloned.1.call-update) | async-done | bytes 3145744 | tf_op jit(solution)/shard_map/all_gather | solution.py:26
  129.4 70.7 %reduce-scatter.13.cloned.1.call-done = f32[32,64]{1,0:T(8,128)} async-done(((f32[512,64]{1,0:T(8,128)}), f32[32,64]{1,0:T(8,128)}) %reduce-scatter.13.cloned.1.call-update) | async-done | bytes 8208 | tf_op jit(solution)/shard_map/reduce_scatter | solution.py:93
  200.9 17.0 %all_gather.32 = bf16[512,64]{1,0:T(8,128)(2,1)S(1)} all-gather(bf16[32,64]{1,0:T(8,128)(2,1)S(1)} %convert_element_type.128), channel_id=1, replica_groups=mesh['store'=8,'mp'=16] {'mp'}, dimensions={0}, use_global_device_ids=true | all-gather | bytes 69632 | tf_op jit(solution)/shard_map/all_gather | solution.py:96
  220.4 12.9 %all-to-all-start.2 = ((bf16[8,64,384]{2,1,0:T(8,128)(2,1)}), bf16[8,64,384]{2,1,0:T(8,128)(2,1)S(1)}, u32[]{:S(2)}, u32[]{:S(2)}) async-start(bf16[8,64,384]{2,1,0:T(8,128)(2,1)} %bitcast.115), calls=%async_computation.2 | async-start | bytes 786432 | tf_op jit(solution)/shard_map/all_to_all | solution.py:106
  233.2 7.7 all-to-all-done.2
  242.8 5.0 fusion.27
  248.0 47.6 %all-gather.13.cloned.1.call-done = bf16[256,6144]{1,0:T(8,128)(2,1)} async-done(((bf16[256,384]{1,0:T(8,128)(2,1)}), bf16[256,6144]{1,0:T(8,128)(2,1)}) %all-gather.13.cloned.1.call-update) | async-done | bytes 3145744 | tf_op jit(solution)/shard_map/all_gather | solution.py:68
  295.6 2.7 fusion.3
  301.2 14.3 %all_to_all.52 = bf16[8,64,384]{2,1,0:T(8,128)(2,1)S(1)} all-to-all(bf16[8,64,384]{2,1,0:T(8,128)(2,1)S(1)} %bitcast.110), channel_id=1, replica_groups=mesh['store'=8,'mp'=16] {'store'}, dimensions={0} | all-to-all | bytes 786432 | tf_op jit(solution)/shard_map/all_to_all | solution.py:77
  318.1 69.2 %reduce-scatter.15.cloned.1.call-done = f32[32,64]{1,0:T(8,128)} async-done(((f32[512,64]{1,0:T(8,128)}), f32[32,64]{1,0:T(8,128)}) %reduce-scatter.15.cloned.1.call-update) | async-done | bytes 8208 | tf_op jit(solution)/shard_map/reduce_scatter | solution.py:93
  388.0 17.0 %all_gather.35 = bf16[512,64]{1,0:T(8,128)(2,1)S(1)} all-gather(bf16[32,64]{1,0:T(8,128)(2,1)S(1)} %convert_element_type.136), channel_id=1, replica_groups=mesh['store'=8,'mp'=16] {'mp'}, dimensions={0}, use_global_device_ids=true | all-gather | bytes 69632 | tf_op jit(solution)/shard_map/all_gather | solution.py:96
  406.7 20.7 %all_to_all.53 = bf16[8,64,384]{2,1,0:T(8,128)(2,1)S(1)} all-to-all(bf16[8,64,384]{2,1,0:T(8,128)(2,1)S(1)} %bitcast.119), channel_id=1, replica_groups=mesh['store'=8,'mp'=16] {'store'}, dimensions={0} | all-to-all | bytes 786432 | tf_op jit(solution)/shard_map/all_to_all | solution.py:106
  429.3 5.0 fusion.26
  434.4 47.4 %all-gather.15.cloned.1.call-done = bf16[256,6144]{1,0:T(8,128)(2,1)} async-done(((bf16[256,384]{1,0:T(8,128)(2,1)}), bf16[256,6144]{1,0:T(8,128)(2,1)}) %all-gather.15.cloned.1.call-update) | async-done | bytes 3145744 | tf_op jit(solution)/shard_map/all_gather | solution.py:68
  481.8 2.7 fusion.6
  487.3 14.3 %all_to_all.54 = bf16[8,64,384]{2,1,0:T(8,128)(2,1)S(1)} all-to-all(bf16[8,64,384]{2,1,0:T(8,128)(2,1)S(1)} %bitcast.111), channel_id=1, replica_groups=mesh['store'=8,'mp'=16] {'store'}, dimensions={0} | all-to-all | bytes 786432 | tf_op jit(solution)/shard_map/all_to_all | solution.py:77
  504.2 69.2 %reduce-scatter.17.cloned.1.call-done = f32[32,64]{1,0:T(8,128)} async-done(((f32[512,64]{1,0:T(8,128)}), f32[32,64]{1,0:T(8,128)}) %reduce-scatter.17.cloned.1.call-update) | async-done | bytes 8208 | tf_op jit(solution)/shard_map/reduce_scatter | solution.py:93
  574.1 17.0 %all_gather.37 = bf16[512,64]{1,0:T(8,128)(2,1)S(1)} all-gather(bf16[32,64]{1,0:T(8,128)(2,1)S(1)} %convert_element_type.143), channel_id=1, replica_groups=mesh['store'=8,'mp'=16] {'mp'}, dimensions={0}, use_global_device_ids=true | all-gather | bytes 69632 | tf_op jit(solution)/shard_map/all_gather | solution.py:96
  592.9 20.7 %all_to_all.55 = bf16[8,64,384]{2,1,0:T(8,128)(2,1)S(1)} all-to-all(bf16[8,64,384]{2,1,0:T(8,128)(2,1)S(1)} %bitcast.121), channel_id=1, replica_groups=mesh['store'=8,'mp'=16] {'store'}, dimensions={0} | all-to-all | bytes 786432 | tf_op jit(solution)/shard_map/all_to_all | solution.py:106
  615.4 5.0 fusion.25
  620.5 47.4 %all-gather.17.cloned.1.call-done = bf16[256,6144]{1,0:T(8,128)(2,1)} async-done(((bf16[256,384]{1,0:T(8,128)(2,1)}), bf16[256,6144]{1,0:T(8,128)(2,1)}) %all-gather.17.cloned.1.call-update) | async-done | bytes 3145744 | tf_op jit(solution)/shard_map/all_gather | solution.py:68
  667.9 2.7 fusion.9
  673.5 14.3 %all_to_all.56 = bf16[8,64,384]{2,1,0:T(8,128)(2,1)S(1)} all-to-all(bf16[8,64,384]{2,1,0:T(8,128)(2,1)S(1)} %bitcast.109), channel_id=1, replica_groups=mesh['store'=8,'mp'=16] {'store'}, dimensions={0} | all-to-all | bytes 786432 | tf_op jit(solution)/shard_map/all_to_all | solution.py:77
  690.3 69.2 %reduce-scatter.19.cloned.1.call-done = f32[32,64]{1,0:T(8,128)} async-done(((f32[512,64]{1,0:T(8,128)}), f32[32,64]{1,0:T(8,128)}) %reduce-scatter.19.cloned.1.call-update) | async-done | bytes 8208 | tf_op jit(solution)/shard_map/reduce_scatter | solution.py:93
  760.2 17.0 %all_gather.39 = bf16[512,64]{1,0:T(8,128)(2,1)S(1)} all-gather(bf16[32,64]{1,0:T(8,128)(2,1)S(1)} %convert_element_type.150), channel_id=1, replica_groups=mesh['store'=8,'mp'=16] {'mp'}, dimensions={0}, use_global_device_ids=true | all-gather | bytes 69632 | tf_op jit(solution)/shard_map/all_gather | solution.py:96
  779.0 20.7 %all_to_all.57 = bf16[8,64,384]{2,1,0:T(8,128)(2,1)S(1)} all-to-all(bf16[8,64,384]{2,1,0:T(8,128)(2,1)S(1)} %bitcast.117), channel_id=1, replica_groups=mesh['store'=8,'mp'=16] {'store'}, dimensions={0} | all-to-all | bytes 786432 | tf_op jit(solution)/shard_map/all_to_all | solution.py:106
  801.5 5.0 fusion.24
  (107 shorter events, 65.5 us)
Async XLA Ops:
  6.5 19.4 %copy-start = (s32[8,4]{0,1:T(4,128)S(1)}, s32[8,4]{0,1:T(4,128)}, u32[]{:S(2)}) copy-start(s32[8,4]{0,1:T(4,128)} %param.13) | copy-start | bytes 388
  6.5 18.6 %copy-start.5 = (bf16[8,64,384]{2,1,0:T(8,128)(2,1)S(1)}, bf16[8,64,384]{2,1,0:T(8,128)(2,1)}, u32[]{:S(2)}) copy-start(bf16[8,64,384]{2,1,0:T(8,128)(2,1)} %param.12) | copy-start | bytes 1179652
  6.5 56.5 %all-gather.7.cloned.1.call-start = ((), (), s32[]{:S(2)}) async-start(), calls=%async_computation.13 | async-start | bytes 3342336 | tf_op jit(solution)/shard_map/all_gather | solution.py:68
  7.3 90.7 %all-gather.9.cloned.1.call-start = ((), (), s32[]{:S(2)}) async-start(), calls=%async_computation.14 | async-start | bytes 3538944 | tf_op jit(solution)/shard_map/all_gather | solution.py:25
  9.3 116.9 %all-gather.11.cloned.1.call-start = ((), (), s32[]{:S(2)}) async-start(), calls=%async_computation.15 | async-start | bytes 3538944 | tf_op jit(solution)/shard_map/all_gather | solution.py:26
  16.6 11.4 %all-to-all-start = ((s32[8,1,64]{2,1,0:T(1,128)}), s32[8,1,64]{2,1,0:T(1,128)S(1)}, u32[]{:S(2)}, u32[]{:S(2)}) async-start(s32[8,1,64]{2,1,0:T(1,128)} %all_to_all.33), calls=%async_computation | async-start | bytes 8192 | tf_op jit(solution)/shard_map/all_to_all | solution.py:78
  63.0 2.8 copy-start.1
  69.9 31.3 %all-to-all-start.1 = ((bf16[8,64,384]{2,1,0:T(8,128)(2,1)}), bf16[8,64,384]{2,1,0:T(8,128)(2,1)S(1)}, u32[]{:S(2)}, u32[]{:S(2)}) async-start(bf16[8,64,384]{2,1,0:T(8,128)(2,1)} %bitcast.6), calls=%async_computation.1 | async-start | bytes 786432 | tf_op jit(solution)/shard_map/all_to_all | solution.py:77
  76.4 123.8 %reduce-scatter.13.cloned.1.call-start = ((), (), s32[]{:S(2)}) async-start(), calls=%async_computation.19 | async-start | bytes 278528 | tf_op jit(solution)/shard_map/reduce_scatter | solution.py:93
  103.5 114.4 %copy-start.9 = (bf16[512,12]{0,1:T(8,128)(2,1)S(1)}, bf16[512,12]{0,1:T(8,128)(2,1)}, u32[]{:S(2)}) copy-start(bf16[512,12]{0,1:T(8,128)(2,1)} %get-tuple-element.5) | copy-start | bytes 36868
  220.4 20.6 %all-to-all-start.2 = ((bf16[8,64,384]{2,1,0:T(8,128)(2,1)}), bf16[8,64,384]{2,1,0:T(8,128)(2,1)S(1)}, u32[]{:S(2)}, u32[]{:S(2)}) async-start(bf16[8,64,384]{2,1,0:T(8,128)(2,1)} %bitcast.115), calls=%async_computation.2 | async-start | bytes 786432 | tf_op jit(solution)/shard_map/all_to_all | solution.py:106
  233.2 62.4 %all-gather.13.cloned.1.call-start = ((), (), s32[]{:S(2)}) async-start(), calls=%async_computation.16 | async-start | bytes 3342336 | tf_op jit(solution)/shard_map/all_gather | solution.py:68
  247.8 50.6 %copy-start.6 = (f32[6144]{0:T(1024)S(1)}, f32[6144]{0:T(1024)}, u32[]{:S(2)}) copy-start(f32[6144]{0:T(1024)} %param.9) | copy-start | bytes 73732
  247.8 139.4 %reduce-scatter.15.cloned.1.call-start = ((), (), s32[]{:S(2)}) async-start(), calls=%async_computation.20 | async-start | bytes 278528 | tf_op jit(solution)/shard_map/reduce_scatter | solution.py:93
  295.6 2.8 copy-start.2
  315.5 89.5 %copy-start.10 = (bf16[512,12]{0,1:T(8,128)(2,1)S(1)}, bf16[512,12]{0,1:T(8,128)(2,1)}, u32[]{:S(2)}) copy-start(bf16[512,12]{0,1:T(8,128)(2,1)} %get-tuple-element.5) | copy-start | bytes 36868
  318.0 163.8 %all-gather.15.cloned.1.call-start = ((), (), s32[]{:S(2)}) async-start(), calls=%async_computation.17 | async-start | bytes 3342336 | tf_op jit(solution)/shard_map/all_gather | solution.py:68
  434.3 50.3 %copy-start.7 = (f32[6144]{0:T(1024)S(1)}, f32[6144]{0:T(1024)}, u32[]{:S(2)}) copy-start(f32[6144]{0:T(1024)} %param.9) | copy-start | bytes 73732
  434.3 139.1 %reduce-scatter.17.cloned.1.call-start = ((), (), s32[]{:S(2)}) async-start(), calls=%async_computation.21 | async-start | bytes 278528 | tf_op jit(solution)/shard_map/reduce_scatter | solution.py:93
  481.8 2.8 copy-start.3
  501.6 89.5 %copy-start.11 = (bf16[512,12]{0,1:T(8,128)(2,1)S(1)}, bf16[512,12]{0,1:T(8,128)(2,1)}, u32[]{:S(2)}) copy-start(bf16[512,12]{0,1:T(8,128)(2,1)} %get-tuple-element.5) | copy-start | bytes 36868
  504.2 163.8 %all-gather.17.cloned.1.call-start = ((), (), s32[]{:S(2)}) async-start(), calls=%async_computation.18 | async-start | bytes 3342336 | tf_op jit(solution)/shard_map/all_gather | solution.py:68
  620.4 50.3 %copy-start.8 = (f32[6144]{0:T(1024)S(1)}, f32[6144]{0:T(1024)}, u32[]{:S(2)}) copy-start(f32[6144]{0:T(1024)} %param.9) | copy-start | bytes 73732
  620.4 139.1 %reduce-scatter.19.cloned.1.call-start = ((), (), s32[]{:S(2)}) async-start(), calls=%async_computation.22 | async-start | bytes 278528 | tf_op jit(solution)/shard_map/reduce_scatter | solution.py:93
  667.9 2.8 copy-start.4
  687.8 89.5 %copy-start.12 = (bf16[512,12]{0,1:T(8,128)(2,1)S(1)}, bf16[512,12]{0,1:T(8,128)(2,1)}, u32[]{:S(2)}) copy-start(bf16[512,12]{0,1:T(8,128)(2,1)} %get-tuple-element.5) | copy-start | bytes 36868
Sparse Core Ops, SparseCore 0:
  9.4 53.5 all-gather.6
  64.7 33.2 all-gather.8
  99.7 26.5 all-gather.10
  129.3 70.8 reduce-scatter.12
  247.9 47.6 all-gather.12
  318.1 69.0 reduce-scatter.14
  434.4 47.3 all-gather.14
  504.3 69.0 reduce-scatter.16
  620.6 47.3 all-gather.16
  690.4 69.0 reduce-scatter.18
where the time goes:
time: 815 us; the launch traced here: 813 us
  waiting for transfers between devices  507 us (62%)
  blocking collectives  173 us (21%)
  matrix products  39.8 us (5%)
  local copies, waits for them, and re-layouts  30.5 us (4%)
  starting transfers between devices  26.6 us (3%)
  other arithmetic  23 us (3%)
  between operations  13.8 us (2%)
    reduce_scatter x4, waiting for transfers between devices, local(): lax.psum_scatter(partial_value, 'mp', scatter_dimension=0, tiled=True)  278 us
    all_gather x4, waiting for transfers between devices, local(): whole = lax.all_gather(state, 'mp', axis=1, tiled=True)  176 us
    all_gather x4, blocking collectives, local(): inner = lax.all_gather(summed_share, 'mp', axis=0, tiled=True)  67.8 us
    all_to_all x3, blocking collectives, local(): lax.all_to_all(outer, 'store', split_axis=0, concat_axis=0, tiled=True)  62.2 us
    all_to_all x3, blocking collectives, local(): lax.all_to_all(row_buffer, 'store', split_axis=0, concat_axis=0, tiled=True)  42.9 us
    all_gather x1, waiting for transfers between devices, local(): lax.all_gather(flattened_down, 'store', axis=0, tiled=True)  21.6 us
    all_gather x1, waiting for transfers between devices, local(): lax.all_gather(flattened_up, 'store', axis=0, tiled=True)  20.9 us
    dot_general x4, matrix products, local(): jnp.dot(normed, base_projection_weight, preferred_element_type=jnp.float32)  20.1 us
  transfers between devices with their start and end apart: 13, of which 12 were waited for; matrix products, arithmetic and copies ran while one was open for 4% of the time, Pallas kernels for 0%

commit v1 on v0

--- a/solution.py
+++ b/solution.py
@@ -65,7 +65,25 @@
     state = tokens
     column_start = lax.axis_index("mp") * width_portion
     for step in range(STEPS):
-        whole = lax.all_gather(state, "mp", axis=1, tiled=True)
+
+        def _begin_wires(axis_key, in_array):
+            degree = lax.axis_size(axis_key)
+            block_list = tuple(((j, (j + 1) % degree) for j in range(degree)))
+            parts_seen = tuple(((j, (j - 1) % degree) for j in range(degree)))
+            known, carry = ([in_array], [in_array])
+            for _ in range(degree // 2):
+                all_rows = lax.ppermute(known[-1], axis_key, block_list)
+                known.append(all_rows)
+            for _ in tuple(range((degree - 1) // 2)):
+                w2 = lax.ppermute(carry[-1], axis_key, parts_seen)
+                carry.append(w2)
+            extra = jnp.concatenate([*known[::-1], *carry[1:]], axis=1)
+            carry_in = jnp.roll(
+                extra, shift=(lax.axis_index(axis_key) - degree // 2) * in_array.shape[1], axis=1
+            )
+            return carry_in
+
+        whole = _begin_wires("mp", state)
         values = whole.astype(jnp.float32)
         mean_sq = jnp.mean(values * values, axis=1, keepdims=True)
         normed = (values * lax.rsqrt(mean_sq + 1e-05) * gain[None, :]).astype(jnp.bfloat16)

time: 815 us -> 901 us (1.11)
  starting transfers between devices: 26.6 us -> 173 us
  waiting for transfers between devices: 507 us -> 412 us
  blocking collectives: 173 us -> 191 us
  other arithmetic: 23 us -> 33.3 us
    all_gather x4 -> x0, waiting for transfers between devices: 176 us -> none  [local(): whole = lax.all_gather(state, 'mp', axis=1, tiled=True)]
    ppermute x0 -> x60, starting transfers between devices: none -> 142 us  [the longest x28 139 us: _begin_wires(): w2 = lax.ppermute(carry[-1], axis_key, parts_seen)]
    ppermute x0 -> x60, waiting for transfers between devices: none -> 119 us  [the longest x32 113 us: _begin_wires(): all_rows = lax.ppermute(known[-1], axis_key, block_list)]
    all_gather x1, waiting for transfers between devices: 21.6 us -> 0.01 us  [local(): lax.all_gather(flattened_down, 'store', axis=0, tiled=True)]
    all_gather x1, waiting for transfers between devices: 20.9 us -> 0.02 us  [local(): lax.all_gather(flattened_up, 'store', axis=0, tiled=True)]
    all_to_all x3, blocking collectives: 42.9 us -> 60.1 us  [local(): lax.all_to_all(row_buffer, 'store', split_axis=0, concat_axis=0, tiled=True)]
  transfers between devices with their start and end apart: 13 -> 69, of which waited for: 12 -> 41; matrix products, arithmetic and copies ran while one was open for 4% -> 4% of each run, Pallas kernels for 0% -> 0%
where the time goes in v1:
time: 901 us; the launch traced here: 894 us
  waiting for transfers between devices  412 us (46%)
  blocking collectives  191 us (21%)
  starting transfers between devices  173 us (19%)
  matrix products  37.8 us (4%)
  other arithmetic  33.3 us (4%)
  local copies, waits for them, and re-layouts  32.8 us (4%)
  between operations  14.7 us (2%)
    reduce_scatter x4, waiting for transfers between devices, local(): lax.psum_scatter(partial_value, 'mp', scatter_dimension=0, tiled=True)  280 us
    ppermute x28, starting transfers between devices, _begin_wires(): w2 = lax.ppermute(carry[-1], axis_key, parts_seen)  139 us
    ppermute x32, waiting for transfers between devices, _begin_wires(): all_rows = lax.ppermute(known[-1], axis_key, block_list)  113 us
    all_gather x4, blocking collectives, local(): inner = lax.all_gather(summed_share, 'mp', axis=0, tiled=True)  68.3 us
    all_to_all x3, blocking collectives, local(): lax.all_to_all(outer, 'store', split_axis=0, concat_axis=0, tiled=True)  62.9 us
    all_to_all x3, blocking collectives, local(): lax.all_to_all(row_buffer, 'store', split_axis=0, concat_axis=0, tiled=True)  60.1 us
  transfers between devices with their start and end apart: 69, of which 41 were waited for; matrix products, arithmetic and copies ran while one was open for 4% of the time, Pallas kernels for 0%

profile of v1, /device:TPU:1, one launch (start us, length us, event | category | flops | bytes accessed | tf_op | source)
XLA Modules:
  0.0 894.0 jit_solution(4918630844477938503)
XLA Ops:
  10.8 8.5 collective-permute-done
  37.4 5.2 collective-permute-start.10
  45.2 5.2 collective-permute-start.11
  54.3 10.8 %all-to-all-start = ((s32[8,1,64]{2,1,0:T(1,128)}), s32[8,1,64]{2,1,0:T(1,128)S(1)}, u32[]{:S(2)}, u32[]{:S(2)}) async-start(s32[8,1,64]{2,1,0:T(1,128)} %all_to_all.33), calls=%async_computation | async-start | bytes 8192 | tf_op jit(solution)/shard_map/all_to_all | solution.py:96
  65.0 5.1 collective-permute-start.12
  74.3 5.5 collective-permute-start.13
  83.1 5.7 collective-permute-start.14
  100.4 6.7 all-to-all-start.1
  122.1 68.2 %reduce-scatter.13.cloned.1.call-done = f32[32,64]{1,0:T(8,128)} async-done(((f32[512,64]{1,0:T(8,128)}), f32[32,64]{1,0:T(8,128)}) %reduce-scatter.13.cloned.1.call-update) | async-done | bytes 8208 | tf_op jit(solution)/shard_map/reduce_scatter | solution.py:111
  191.1 17.2 %all_gather.19 = bf16[512,64]{1,0:T(8,128)(2,1)S(1)} all-gather(bf16[32,64]{1,0:T(8,128)(2,1)S(1)} %convert_element_type.128), channel_id=1, replica_groups=mesh['store'=8,'mp'=16] {'mp'}, dimensions={0}, use_global_device_ids=true | all-gather | bytes 69632 | tf_op jit(solution)/shard_map/all_gather | solution.py:114
  210.8 12.9 %all-to-all-start.2 = ((bf16[8,64,384]{2,1,0:T(8,128)(2,1)}), bf16[8,64,384]{2,1,0:T(8,128)(2,1)S(1)}, u32[]{:S(2)}, u32[]{:S(2)}) async-start(bf16[8,64,384]{2,1,0:T(8,128)(2,1)} %bitcast.110), calls=%async_computation.2 | async-start | bytes 786432 | tf_op jit(solution)/shard_map/all_to_all | solution.py:124
  223.9 7.5 all-to-all-done.2
  237.6 8.5 collective-permute-done.15
  285.6 5.1 collective-permute-start.28
  295.0 5.6 collective-permute-start.29
  313.7 20.3 %all_to_all.52 = bf16[8,64,384]{2,1,0:T(8,128)(2,1)S(1)} all-to-all(bf16[8,64,384]{2,1,0:T(8,128)(2,1)S(1)} %bitcast.105), channel_id=1, replica_groups=mesh['store'=8,'mp'=16] {'store'}, dimensions={0} | all-to-all | bytes 786432 | tf_op jit(solution)/shard_map/all_to_all | solution.py:95
  336.5 71.0 %reduce-scatter.15.cloned.1.call-done = f32[32,64]{1,0:T(8,128)} async-done(((f32[512,64]{1,0:T(8,128)}), f32[32,64]{1,0:T(8,128)}) %reduce-scatter.15.cloned.1.call-update) | async-done | bytes 8208 | tf_op jit(solution)/shard_map/reduce_scatter | solution.py:111
  408.2 17.2 %all_gather.21 = bf16[512,64]{1,0:T(8,128)(2,1)S(1)} all-gather(bf16[32,64]{1,0:T(8,128)(2,1)S(1)} %convert_element_type.136), channel_id=1, replica_groups=mesh['store'=8,'mp'=16] {'mp'}, dimensions={0}, use_global_device_ids=true | all-gather | bytes 69632 | tf_op jit(solution)/shard_map/all_gather | solution.py:114
  427.2 20.9 %all_to_all.53 = bf16[8,64,384]{2,1,0:T(8,128)(2,1)S(1)} all-to-all(bf16[8,64,384]{2,1,0:T(8,128)(2,1)S(1)} %bitcast.114), channel_id=1, replica_groups=mesh['store'=8,'mp'=16] {'store'}, dimensions={0} | all-to-all | bytes 786432 | tf_op jit(solution)/shard_map/all_to_all | solution.py:124
  454.3 8.9 collective-permute-done.30
  511.3 5.4 collective-permute-start.44
  530.5 19.9 %all_to_all.54 = bf16[8,64,384]{2,1,0:T(8,128)(2,1)S(1)} all-to-all(bf16[8,64,384]{2,1,0:T(8,128)(2,1)S(1)} %bitcast.106), channel_id=1, replica_groups=mesh['store'=8,'mp'=16] {'store'}, dimensions={0} | all-to-all | bytes 786432 | tf_op jit(solution)/shard_map/all_to_all | solution.py:95
  553.0 70.6 %reduce-scatter.17.cloned.1.call-done = f32[32,64]{1,0:T(8,128)} async-done(((f32[512,64]{1,0:T(8,128)}), f32[32,64]{1,0:T(8,128)}) %reduce-scatter.17.cloned.1.call-update) | async-done | bytes 8208 | tf_op jit(solution)/shard_map/reduce_scatter | solution.py:111
  624.3 17.0 %all_gather.22 = bf16[512,64]{1,0:T(8,128)(2,1)S(1)} all-gather(bf16[32,64]{1,0:T(8,128)(2,1)S(1)} %convert_element_type.143), channel_id=1, replica_groups=mesh['store'=8,'mp'=16] {'mp'}, dimensions={0}, use_global_device_ids=true | all-gather | bytes 69632 | tf_op jit(solution)/shard_map/all_gather | solution.py:114
  643.1 21.1 %all_to_all.55 = bf16[8,64,384]{2,1,0:T(8,128)(2,1)S(1)} all-to-all(bf16[8,64,384]{2,1,0:T(8,128)(2,1)S(1)} %bitcast.116), channel_id=1, replica_groups=mesh['store'=8,'mp'=16] {'store'}, dimensions={0} | all-to-all | bytes 786432 | tf_op jit(solution)/shard_map/all_to_all | solution.py:124
  670.5 8.9 collective-permute-done.45
  727.5 5.4 collective-permute-start.59
  746.6 19.9 %all_to_all.56 = bf16[8,64,384]{2,1,0:T(8,128)(2,1)S(1)} all-to-all(bf16[8,64,384]{2,1,0:T(8,128)(2,1)S(1)} %bitcast.104), channel_id=1, replica_groups=mesh['store'=8,'mp'=16] {'store'}, dimensions={0} | all-to-all | bytes 786432 | tf_op jit(solution)/shard_map/all_to_all | solution.py:95
  769.1 70.6 %reduce-scatter.19.cloned.1.call-done = f32[32,64]{1,0:T(8,128)} async-done(((f32[512,64]{1,0:T(8,128)}), f32[32,64]{1,0:T(8,128)}) %reduce-scatter.19.cloned.1.call-update) | async-done | bytes 8208 | tf_op jit(solution)/shard_map/reduce_scatter | solution.py:111
  840.4 17.0 %all_gather.23 = bf16[512,64]{1,0:T(8,128)(2,1)S(1)} all-gather(bf16[32,64]{1,0:T(8,128)(2,1)S(1)} %convert_element_type.150), channel_id=1, replica_groups=mesh['store'=8,'mp'=16] {'mp'}, dimensions={0}, use_global_device_ids=true | all-gather | bytes 69632 | tf_op jit(solution)/shard_map/all_gather | solution.py:114
  859.2 20.9 %all_to_all.57 = bf16[8,64,384]{2,1,0:T(8,128)(2,1)S(1)} all-to-all(bf16[8,64,384]{2,1,0:T(8,128)(2,1)S(1)} %bitcast.112), channel_id=1, replica_groups=mesh['store'=8,'mp'=16] {'store'}, dimensions={0} | all-to-all | bytes 786432 | tf_op jit(solution)/shard_map/all_to_all | solution.py:124
  881.9 5.0 fusion.28
  (281 shorter events, 281.7 us)
Async XLA Ops:
  6.5 100.6 %all-gather.3.cloned.1.call-start = ((), (), s32[]{:S(2)}) async-start(), calls=%async_computation.13 | async-start | bytes 3538944 | tf_op jit(solution)/shard_map/all_gather | solution.py:25
  8.7 110.3 %all-gather.5.cloned.1.call-start = ((), (), s32[]{:S(2)}) async-start(), calls=%async_computation.14 | async-start | bytes 3538944 | tf_op jit(solution)/shard_map/all_gather | solution.py:26
  8.7 10.6 %collective-permute-start = (bf16[256,384]{1,0:T(8,128)(2,1)}, bf16[256,384]{1,0:T(8,128)(2,1)S(1)}, u32[]{:S(2)}, u32[]{:S(2)}) collective-permute-start(bf16[256,384]{1,0:T(8,128)(2,1)} %param.10), channel_id=1, source_target_pairs={{0,1},{1,2},{2,3},{3,4},{4,5},{5,6},{6,7},{7,8},{8,9},{9,10},{10,1... | collective-permute-start | bytes 589832 | tf_op jit(solution)/shard_map/ppermute | solution.py:75
  19.3 10.6 %collective-permute-start.8 = (bf16[256,384]{1,0:T(8,128)(2,1)}, bf16[256,384]{1,0:T(8,128)(2,1)S(1)}, u32[]{:S(2)}, u32[]{:S(2)}) collective-permute-start(bf16[256,384]{1,0:T(8,128)(2,1)} %param.10), channel_id=1, source_target_pairs={{0,15},{1,0},{2,1},{3,2},{4,3},{5,4},{6,5},{7,6},{8,7},{9,8},{10,9... | collective-permute-start | bytes 589832 | tf_op jit(solution)/shard_map/ppermute | solution.py:78
  45.2 19.9 %collective-permute-start.11 = (bf16[256,384]{1,0:T(8,128)(2,1)S(1)}, bf16[256,384]{1,0:T(8,128)(2,1)S(1)}, u32[]{:S(2)}, u32[]{:S(2)}) collective-permute-start(bf16[256,384]{1,0:T(8,128)(2,1)S(1)} %collective-permute-done.10), channel_id=1, source_target_pairs={{0,15},{1,0},{2,1},{3,2},{4,3},{5,4},{6,5},{7,6},{8,7},{9,8},{10,9... | collective-permute-start | bytes 589832 | tf_op jit(solution)/shard_map/ppermute | solution.py:78
  51.3 18.8 %collective-permute-start.5 = (bf16[256,384]{1,0:T(8,128)(2,1)S(1)}, bf16[256,384]{1,0:T(8,128)(2,1)S(1)}, u32[]{:S(2)}, u32[]{:S(2)}) collective-permute-start(bf16[256,384]{1,0:T(8,128)(2,1)S(1)} %collective-permute-done.4), channel_id=1, source_target_pairs={{0,1},{1,2},{2,3},{3,4},{4,5},{5,6},{6,7},{7,8},{8,9},{9,10},{10,1... | collective-permute-start | bytes 589832 | tf_op jit(solution)/shard_map/ppermute | solution.py:75
  54.3 18.6 %all-to-all-start = ((s32[8,1,64]{2,1,0:T(1,128)}), s32[8,1,64]{2,1,0:T(1,128)S(1)}, u32[]{:S(2)}, u32[]{:S(2)}) async-start(s32[8,1,64]{2,1,0:T(1,128)} %all_to_all.33), calls=%async_computation | async-start | bytes 8192 | tf_op jit(solution)/shard_map/all_to_all | solution.py:96
  65.0 9.2 %collective-permute-start.12 = (bf16[256,384]{1,0:T(8,128)(2,1)S(1)}, bf16[256,384]{1,0:T(8,128)(2,1)S(1)}, u32[]{:S(2)}, u32[]{:S(2)}) collective-permute-start(bf16[256,384]{1,0:T(8,128)(2,1)S(1)} %collective-permute-done.11), channel_id=1, source_target_pairs={{0,15},{1,0},{2,1},{3,2},{4,3},{5,4},{6,5},{7,6},{8,7},{9,8},{10,9... | collective-permute-start | bytes 589832 | tf_op jit(solution)/shard_map/ppermute | solution.py:78
  70.1 9.7 %collective-permute-start.6 = (bf16[256,384]{1,0:T(8,128)(2,1)S(1)}, bf16[256,384]{1,0:T(8,128)(2,1)S(1)}, u32[]{:S(2)}, u32[]{:S(2)}) collective-permute-start(bf16[256,384]{1,0:T(8,128)(2,1)S(1)} %collective-permute-done.5), channel_id=1, source_target_pairs={{0,1},{1,2},{2,3},{3,4},{4,5},{5,6},{6,7},{7,8},{8,9},{9,10},{10,1... | collective-permute-start | bytes 589832 | tf_op jit(solution)/shard_map/ppermute | solution.py:75
  74.3 8.8 collective-permute-start.13
  79.8 9.0 %collective-permute-start.7 = (bf16[256,384]{1,0:T(8,128)(2,1)S(1)}, bf16[256,384]{1,0:T(8,128)(2,1)S(1)}, u32[]{:S(2)}, u32[]{:S(2)}) collective-permute-start(bf16[256,384]{1,0:T(8,128)(2,1)S(1)} %collective-permute-done.6), channel_id=1, source_target_pairs={{0,1},{1,2},{2,3},{3,4},{4,5},{5,6},{6,7},{7,8},{8,9},{9,10},{10,1... | collective-permute-start | bytes 589832 | tf_op jit(solution)/shard_map/ppermute | solution.py:75
  100.4 14.4 %all-to-all-start.1 = ((bf16[8,64,384]{2,1,0:T(8,128)(2,1)}), bf16[8,64,384]{2,1,0:T(8,128)(2,1)S(1)}, u32[]{:S(2)}, u32[]{:S(2)}) async-start(bf16[8,64,384]{2,1,0:T(8,128)(2,1)} %bitcast.6), calls=%async_computation.1 | async-start | bytes 786432 | tf_op jit(solution)/shard_map/all_to_all | solution.py:95
  107.1 83.3 %reduce-scatter.13.cloned.1.call-start = ((), (), s32[]{:S(2)}) async-start(), calls=%async_computation.15 | async-start | bytes 278528 | tf_op jit(solution)/shard_map/reduce_scatter | solution.py:111
  210.8 20.6 %all-to-all-start.2 = ((bf16[8,64,384]{2,1,0:T(8,128)(2,1)}), bf16[8,64,384]{2,1,0:T(8,128)(2,1)S(1)}, u32[]{:S(2)}, u32[]{:S(2)}) async-start(bf16[8,64,384]{2,1,0:T(8,128)(2,1)} %bitcast.110), calls=%async_computation.2 | async-start | bytes 786432 | tf_op jit(solution)/shard_map/all_to_all | solution.py:124
  223.7 183.8 %reduce-scatter.15.cloned.1.call-start = ((), (), s32[]{:S(2)}) async-start(), calls=%async_computation.16 | async-start | bytes 278528 | tf_op jit(solution)/shard_map/reduce_scatter | solution.py:111
  237.5 8.6 collective-permute-start.15
  285.6 9.2 %collective-permute-start.21 = (bf16[256,384]{1,0:T(8,128)(2,1)S(1)}, bf16[256,384]{1,0:T(8,128)(2,1)S(1)}, u32[]{:S(2)}, u32[]{:S(2)}) collective-permute-start(bf16[256,384]{1,0:T(8,128)(2,1)S(1)} %collective-permute-done.20), channel_id=1, source_target_pairs={{0,1},{1,2},{2,3},{3,4},{4,5},{5,6},{6,7},{7,8},{8,9},{9,10},{10,1... | collective-permute-start | bytes 589832 | tf_op jit(solution)/shard_map/ppermute | solution.py:75
  285.6 9.4 %collective-permute-start.28 = (bf16[256,384]{1,0:T(8,128)(2,1)S(1)}, bf16[256,384]{1,0:T(8,128)(2,1)S(1)}, u32[]{:S(2)}, u32[]{:S(2)}) collective-permute-start(bf16[256,384]{1,0:T(8,128)(2,1)S(1)} %collective-permute-done.27), channel_id=1, source_target_pairs={{0,15},{1,0},{2,1},{3,2},{4,3},{5,4},{6,5},{7,6},{8,7},{9,8},{10,9... | collective-permute-start | bytes 589832 | tf_op jit(solution)/shard_map/ppermute | solution.py:78
  294.9 9.8 %collective-permute-start.22 = (bf16[256,384]{1,0:T(8,128)(2,1)S(1)}, bf16[256,384]{1,0:T(8,128)(2,1)S(1)}, u32[]{:S(2)}, u32[]{:S(2)}) collective-permute-start(bf16[256,384]{1,0:T(8,128)(2,1)S(1)} %collective-permute-done.21), channel_id=1, source_target_pairs={{0,1},{1,2},{2,3},{3,4},{4,5},{5,6},{6,7},{7,8},{8,9},{9,10},{10,1... | collective-permute-start | bytes 589832 | tf_op jit(solution)/shard_map/ppermute | solution.py:75
  295.0 10.4 %collective-permute-start.29 = (bf16[256,384]{1,0:T(8,128)(2,1)S(1)}, bf16[256,384]{1,0:T(8,128)(2,1)S(1)}, u32[]{:S(2)}, u32[]{:S(2)}) collective-permute-start(bf16[256,384]{1,0:T(8,128)(2,1)S(1)} %collective-permute-done.28), channel_id=1, source_target_pairs={{0,15},{1,0},{2,1},{3,2},{4,3},{5,4},{6,5},{7,6},{8,7},{9,8},{10,9... | collective-permute-start | bytes 589832 | tf_op jit(solution)/shard_map/ppermute | solution.py:78
  336.5 287.1 %reduce-scatter.17.cloned.1.call-start = ((), (), s32[]{:S(2)}) async-start(), calls=%async_computation.17 | async-start | bytes 278528 | tf_op jit(solution)/shard_map/reduce_scatter | solution.py:111
  454.2 9.0 %collective-permute-start.30 = (bf16[256,384]{1,0:T(8,128)(2,1)S(1)}, bf16[256,384]{1,0:T(8,128)(2,1)S(1)}, u32[]{:S(2)}, u32[]{:S(2)}) collective-permute-start(bf16[256,384]{1,0:T(8,128)(2,1)S(1)} %fusion.30), channel_id=1, source_target_pairs={{0,1},{1,2},{2,3},{3,4},{4,5},{5,6},{6,7},{7,8},{8,9},{9,10},{10,1... | collective-permute-start | bytes 589832 | tf_op jit(solution)/shard_map/ppermute | solution.py:75
  502.4 8.9 collective-permute-start.36
  502.4 8.9 collective-permute-start.43
  511.3 10.2 %collective-permute-start.37 = (bf16[256,384]{1,0:T(8,128)(2,1)S(1)}, bf16[256,384]{1,0:T(8,128)(2,1)S(1)}, u32[]{:S(2)}, u32[]{:S(2)}) collective-permute-start(bf16[256,384]{1,0:T(8,128)(2,1)S(1)} %collective-permute-done.36), channel_id=1, source_target_pairs={{0,1},{1,2},{2,3},{3,4},{4,5},{5,6},{6,7},{7,8},{8,9},{9,10},{10,1... | collective-permute-start | bytes 589832 | tf_op jit(solution)/shard_map/ppermute | solution.py:75
  511.3 10.8 %collective-permute-start.44 = (bf16[256,384]{1,0:T(8,128)(2,1)S(1)}, bf16[256,384]{1,0:T(8,128)(2,1)S(1)}, u32[]{:S(2)}, u32[]{:S(2)}) collective-permute-start(bf16[256,384]{1,0:T(8,128)(2,1)S(1)} %collective-permute-done.43), channel_id=1, source_target_pairs={{0,15},{1,0},{2,1},{3,2},{4,3},{5,4},{6,5},{7,6},{8,7},{9,8},{10,9... | collective-permute-start | bytes 589832 | tf_op jit(solution)/shard_map/ppermute | solution.py:78
  552.9 286.8 %reduce-scatter.19.cloned.1.call-start = ((), (), s32[]{:S(2)}) async-start(), calls=%async_computation.18 | async-start | bytes 278528 | tf_op jit(solution)/shard_map/reduce_scatter | solution.py:111
  670.4 9.0 %collective-permute-start.45 = (bf16[256,384]{1,0:T(8,128)(2,1)S(1)}, bf16[256,384]{1,0:T(8,128)(2,1)S(1)}, u32[]{:S(2)}, u32[]{:S(2)}) collective-permute-start(bf16[256,384]{1,0:T(8,128)(2,1)S(1)} %fusion.29), channel_id=1, source_target_pairs={{0,1},{1,2},{2,3},{3,4},{4,5},{5,6},{6,7},{7,8},{8,9},{9,10},{10,1... | collective-permute-start | bytes 589832 | tf_op jit(solution)/shard_map/ppermute | solution.py:75
  718.6 8.9 collective-permute-start.51
  718.6 8.9 collective-permute-start.58
  727.5 10.1 %collective-permute-start.52 = (bf16[256,384]{1,0:T(8,128)(2,1)S(1)}, bf16[256,384]{1,0:T(8,128)(2,1)S(1)}, u32[]{:S(2)}, u32[]{:S(2)}) collective-permute-start(bf16[256,384]{1,0:T(8,128)(2,1)S(1)} %collective-permute-done.51), channel_id=1, source_target_pairs={{0,1},{1,2},{2,3},{3,4},{4,5},{5,6},{6,7},{7,8},{8,9},{9,10},{10,1... | collective-permute-start | bytes 589832 | tf_op jit(solution)/shard_map/ppermute | solution.py:75
  727.5 10.8 %collective-permute-start.59 = (bf16[256,384]{1,0:T(8,128)(2,1)S(1)}, bf16[256,384]{1,0:T(8,128)(2,1)S(1)}, u32[]{:S(2)}, u32[]{:S(2)}) collective-permute-start(bf16[256,384]{1,0:T(8,128)(2,1)S(1)} %collective-permute-done.58), channel_id=1, source_target_pairs={{0,15},{1,0},{2,1},{3,2},{4,3},{5,4},{6,5},{7,6},{8,7},{9,8},{10,9... | collective-permute-start | bytes 589832 | tf_op jit(solution)/shard_map/ppermute | solution.py:78
  (51 other events, 1088.9 us)
Sparse Core Ops, SparseCore 0:
  9.0 31.4 all-gather.2
  42.2 27.6 all-gather.4
  119.0 71.2 reduce-scatter.12
  336.6 70.8 reduce-scatter.14
  553.0 70.5 reduce-scatter.16
  769.2 70.4 reduce-scatter.18
